TPU v7x, 256 devices: a whole 4x4x8 slice. The times are simulated.
256 devices in a mesh: blk: 32 (over x, z_lo, core), grp: 8 (over y, z_hi).
Axes of the slice: x: 4, y: 4, z: 8 (z_hi: 2, z_lo: 4; z = z_hi * 4 + z_lo), core: 2. Of those that a mesh axis runs over, the one named last changes fastest.
Arguments:
- activations: bfloat16 [16384, 8192], P('blk', 'grp'), may hold values from -6 to 6
- output_grads: bfloat16 [16384, 28672], P('blk', 'grp'), may hold values from -6 to 6
- query_left: bfloat16 [64, 32, 8192], P('blk', None, 'grp'), may hold values from -0.0078125 to 0.0078125
- query_right: bfloat16 [64, 32, 28672], P('blk', None, 'grp'), may hold values from -0.00390625 to 0.00390625
- basis_inputs: bfloat16 [32, 8192, 256], P('blk', 'grp'), may hold values from -0.0625 to 0.0625
- eigen_inputs: bfloat16 [32, 256], P('blk'), may hold values from 0.099609375 to 100
- basis_outputs: bfloat16 [32, 28672, 512], P('blk', 'grp'), may hold values from -0.03125 to 0.03125
- eigen_outputs: bfloat16 [32, 512], P('blk'), may hold values from 0.099609375 to 100
- owners: int32 [2], replicated, may hold values from 0 to 31
- seq_lengths: int32 [128], P('blk'), may hold values from 1 to 128, as said below
Outputs:
- scores: float32 [128, 64], P('blk')
Inputs may be any that keep to these rules, and one draw needn't show every extreme that they name: `seq_lengths`: the 4 lengths of one shard sum to at most 512; in every draw some shard is full (all its lengths 128) and some sequence has length 1.
All inputs are finite; a program needn't handle non-finite values.
Results may differ from a plain program's by a relative error of at most 0.02.
Values may be sent and summed in bfloat16 or wider, within the bound.
No kernel may reach another device: no remote copies, remote signals or barrier semaphores. Data moves between devices by JAX's collectives and lax.ppermute only.
A program may use at most 128 MiB of HBM per device.

v0:
```python
import jax
import jax.numpy as jnp
from jax import lax
from jax.sharding import PartitionSpec as P


def broadcast(x, axis, root):
    mine = lax.axis_index(axis) == root
    return lax.psum(jnp.where(mine, x, jnp.zeros_like(x)), axis)


def contract(row_block, factors):
    return lax.dot_general(
        row_block, factors, (((1,), (1,)), ((), ())), preferred_element_type=jnp.float32
    )


def finish(flat_rows, coeffs, basis, eigen):
    eigen_float = eigen.astype(jnp.float32)
    damped = (coeffs * (eigen_float / (1.0 + eigen_float))).astype(jnp.bfloat16)
    return (flat_rows.astype(jnp.float32) - contract(damped, basis)).astype(jnp.bfloat16)


def membership(seq_lens, slot_count):
    seq_ends = jnp.cumsum(seq_lens)
    seq_starts = seq_ends - seq_lens
    position = jnp.arange(slot_count, dtype=jnp.int32)[None, :]
    inside = (position >= seq_starts[:, None]) & (position < seq_ends[:, None])
    return inside.astype(jnp.float32)


def pair_scores(sum_left, sum_right, query_rank):
    product = (sum_left * sum_right).reshape(sum_left.shape[0], -1, query_rank)
    return jnp.sum(product, axis=2)


def local(
    activations,
    output_grads,
    query_left,
    query_right,
    basis_inputs,
    eigen_inputs,
    basis_outputs,
    eigen_outputs,
    owners,
    seq_lengths,
):
    basis_left, eigen_left = (
        broadcast(basis_inputs[0], "blk", owners[0]),
        broadcast(eigen_inputs[0], "blk", owners[0]),
    )
    basis_right, eigen_right = (
        broadcast(basis_outputs[0], "blk", owners[1]),
        broadcast(eigen_outputs[0], "blk", owners[1]),
    )
    query_rank = query_left.shape[1]
    left_flat = query_left.reshape(-1, query_left.shape[2])
    right_flat = query_right.reshape(-1, query_right.shape[2])
    left_coeffs = jnp.dot(left_flat, basis_left, preferred_element_type=jnp.float32)
    right_coeffs = jnp.dot(right_flat, basis_right, preferred_element_type=jnp.float32)
    left_coeffs, right_coeffs = (
        lax.psum(left_coeffs.astype(jnp.bfloat16), "grp").astype(jnp.float32),
        lax.psum(right_coeffs.astype(jnp.bfloat16), "grp").astype(jnp.float32),
    )
    left_ready = finish(left_flat, left_coeffs, basis_left, eigen_left).reshape(query_left.shape)
    right_ready = finish(right_flat, right_coeffs, basis_right, eigen_right).reshape(
        query_right.shape
    )
    slot_count = activations.shape[0]
    pieces = (
        lax.all_gather(left_ready, "blk", axis=0, tiled=True),
        lax.all_gather(right_ready, "blk", axis=0, tiled=True),
    )
    left_piece = pieces[0].reshape(-1, pieces[0].shape[2])
    right_piece = pieces[1].reshape(-1, pieces[1].shape[2])
    new_left = contract(activations, left_piece)
    new_right = contract(output_grads, right_piece)
    member = membership(seq_lengths, slot_count)
    sum_left, sum_right = (
        lax.psum(new_left.astype(jnp.bfloat16), "grp").astype(jnp.float32),
        lax.psum(new_right.astype(jnp.bfloat16), "grp").astype(jnp.float32),
    )
    result = jnp.dot(
        member,
        pair_scores(sum_left, sum_right, query_rank),
        precision=lax.Precision.HIGHEST,
        preferred_element_type=jnp.float32,
    )
    return result


def solution(mesh):
    in_specs = (
        P("blk", "grp"),
        P("blk", "grp"),
        P("blk", None, "grp"),
        P("blk", None, "grp"),
        P("blk", "grp", None),
        P("blk", None),
        P("blk", "grp", None),
        P("blk", None),
        P(),
        P("blk"),
    )
    out_specs = P("blk", None)
    return jax.shard_map(local, mesh=mesh, in_specs=in_specs, out_specs=out_specs, check_vma=False)
```

profile of v0, /device:TPU:1, one launch (start us, length us, event | category | flops | bytes accessed | tf_op | source)
XLA Modules:
  0.0 944.6 jit_solution(18013591543518392698)
XLA Ops:
  6.5 1.4 fusion.15
  9.2 2.1 select_bitcast_fusion
  11.3 0.9 select_bitcast_fusion.1
  12.2 0.0 all-reduce.7.cloned.1.call-start
  12.4 70.3 %all-reduce = (bf16[512]{0:T(512)(128)(2,1)S(1)}, bf16[256]{0:T(256)(128)(2,1)S(1)}) all-reduce(bf16[512]{0:T(512)(128)(2,1)S(1)} %fusion.13, bf16[256]{0:T(256)(128)(2,1)S(1)} %fusion.14), channel_id=1, replica_groups=mesh['blk'=32,'grp'=8] {'blk'}, use_global_device_ids=true, to_apply=%region_7.8 | all-reduce | flops 768 | bytes 3072 | tf_op jit(solution)/shard_map/psum | solution.py:9
  82.7 227.5 %all-reduce.9.cloned.1.call-done = (bf16[3584,512]{1,0:T(8,128)(2,1)}, bf16[1024,256]{1,0:T(8,128)(2,1)}) async-done(((bf16[3584,512]{1,0:T(8,128)(2,1)}, bf16[1024,256]{1,0:T(8,128)(2,1)}), (bf16[3584,512]{1,0:T(8,128)(2,1)}, bf16[1024,256]{1,0:T(8,128)(2,1)})) %all-reduce.9.cloned.1.call-update) | async-done | bytes 4194320 | tf_op jit(solution)/shard_map/psum | solution.py:9
  310.2 3.9 fusion.4
  314.2 0.0 all-gather.3.cloned.1.call-start
  314.2 0.3 fusion.5
  314.6 44.7 %psum.57 = bf16[64,256]{0,1:T(8,128)(2,1)S(1)} all-reduce(bf16[64,256]{0,1:T(8,128)(2,1)S(1)} %fusion.5), channel_id=1, replica_groups=mesh['blk'=32,'grp'=8] {'grp'}, use_global_device_ids=true, to_apply=%region_2.3 | all-reduce | flops 16384 | bytes 65536 | tf_op jit(solution)/shard_map/psum | solution.py:63
  359.3 1.0 fusion.3
  360.3 0.0 all-gather.5.cloned.1.call-start
  360.4 53.4 %all-reduce.7.cloned.1.call-done = bf16[64,512]{0,1:T(8,128)(2,1)} async-done(((bf16[64,512]{0,1:T(8,128)(2,1)}), bf16[64,512]{0,1:T(8,128)(2,1)}) %all-reduce.7.cloned.1.call-update) | async-done | bytes 65552 | tf_op jit(solution)/shard_map/psum | solution.py:64
  413.7 4.3 fusion
  418.0 0.0 all-reduce.11.cloned.1.call-start
  418.1 60.6 %all-gather.3.cloned.1.call-done = bf16[64,32,1024]{2,1,0:T(8,128)(2,1)} async-done(((bf16[2,32,1024]{2,1,0:T(8,128)(2,1)}), bf16[64,32,1024]{2,1,0:T(8,128)(2,1)}) %all-gather.3.cloned.1.call-update) | async-done | bytes 4194320 | tf_op jit(solution)/shard_map/all_gather | solution.py:72
  478.6 5.9 fusion.2
  484.5 83.8 %all-gather.5.cloned.1.call-done = bf16[64,32,3584]{2,1,0:T(8,128)(2,1)} async-done(((bf16[2,32,3584]{2,1,0:T(8,128)(2,1)}), bf16[64,32,3584]{2,1,0:T(8,128)(2,1)}) %all-gather.5.cloned.1.call-update) | async-done | bytes 14680080 | tf_op jit(solution)/shard_map/all_gather | solution.py:73
  568.3 13.1 %fusion.1 = bf16[512,2048]{0,1:T(8,128)(2,1)} fusion(bf16[2048,3584]{1,0:T(8,128)(2,1)} %bitcast.43, bf16[512,3584]{1,0:T(8,128)(2,1)} %param.11), kind=kOutput, calls=%fused_computation.7 | convolution fusion | flops 7517241344 | bytes 20447232 | tf_op jit(solution)/shard_map/dot_general | solution.py:13
  581.4 0.6 copy-done.7
  582.1 0.2 reduce-window.8
  582.2 351.7 %all-reduce.11.cloned.1.call-done = (bf16[512,2048]{0,1:T(8,128)(2,1)}, bf16[512,2048]{0,1:T(8,128)(2,1)}) async-done(((bf16[512,2048]{0,1:T(8,128)(2,1)}, bf16[512,2048]{0,1:T(8,128)(2,1)}), (bf16[512,2048]{0,1:T(8,128)(2,1)}, bf16[512,2048]{0,1:T(8,128)(2,1)})) %all-reduce.11.cloned.1.call-update) | async-done | bytes 4194320 | tf_op jit(solution)/shard_map/psum | solution.py:82
  934.0 3.3 bitcast_reduce_fusion
  937.2 0.8 fusion.9
  (26 shorter events, 0.2 us)
Async XLA Ops:
  6.5 472.1 %copy-start = (bf16[512,1024]{1,0:T(8,128)(2,1)S(1)}, bf16[512,1024]{1,0:T(8,128)(2,1)}, u32[]{:S(2)}) copy-start(bf16[512,1024]{1,0:T(8,128)(2,1)} %param.10) | copy-start | bytes 3145732
  6.5 303.7 %all-reduce.9.cloned.1.call-start = ((), (), s32[]{:S(2)}) async-start(), calls=%async_computation.3 | async-start | bytes 8388608 | tf_op jit(solution)/shard_map/psum | solution.py:9
  9.2 2.1 copy-start.2
  11.3 1.0 copy-start.6
  11.3 1.0 copy-start.5
  11.3 298.9 %copy-start.4 = (bf16[2,32,3584]{2,1,0:T(8,128)(2,1)S(1)}, bf16[2,32,3584]{2,1,0:T(8,128)(2,1)}, u32[]{:S(2)}) copy-start(bf16[2,32,3584]{2,1,0:T(8,128)(2,1)} %param.13) | copy-start | bytes 1376260
  12.2 302.0 %copy-start.3 = (bf16[2,32,1024]{2,1,0:T(8,128)(2,1)S(1)}, bf16[2,32,1024]{2,1,0:T(8,128)(2,1)}, u32[]{:S(2)}) copy-start(bf16[2,32,1024]{2,1,0:T(8,128)(2,1)} %param.12) | copy-start | bytes 393220
  12.2 401.5 %all-reduce.7.cloned.1.call-start = ((), (), s32[]{:S(2)}) async-start(), calls=%async_computation.1 | async-start | bytes 262144 | tf_op jit(solution)/shard_map/psum | solution.py:64
  310.2 4.0 copy-start.1
  314.2 164.5 %all-gather.3.cloned.1.call-start = ((), (), s32[]{:S(2)}) async-start(), calls=%async_computation | async-start | bytes 4325376 | tf_op jit(solution)/shard_map/all_gather | solution.py:72
  360.3 208.0 %all-gather.5.cloned.1.call-start = ((), (), s32[]{:S(2)}) async-start(), calls=%async_computation.2 | async-start | bytes 15138816 | tf_op jit(solution)/shard_map/all_gather | solution.py:73
  418.0 515.9 %all-reduce.11.cloned.1.call-start = ((), (), s32[]{:S(2)}) async-start(), calls=%async_computation.4 | async-start | bytes 8388608 | tf_op jit(solution)/shard_map/psum | solution.py:82
  581.4 0.7 copy-start.7
Sparse Core Ops, SparseCore 0:
  12.4 297.7 all-reduce.8
  314.3 99.4 all-reduce.6
  415.6 62.9 all-gather.2
  480.3 87.9 all-gather.4
  581.5 352.3 all-reduce.10
where the time goes:
time: 945 us
  waiting for transfers between devices  777 us (82%)
  blocking collectives  115 us (12%)
  matrix products  29.3 us (3%)
  between operations  14.5 us (2%)
    psum x1, waiting for transfers between devices, local(): lax.psum(new_right.astype(jnp.bfloat16), 'grp').astype(jnp.float32)  352 us
    psum x1, waiting for transfers between devices, broadcast(): return lax.psum(jnp.where(mine, x, jnp.zeros_like(x)), axis)  228 us
    all_gather x1, waiting for transfers between devices, local(): lax.all_gather(right_ready, 'blk', axis=0, tiled=True)  83.8 us
    psum x1, blocking collectives, broadcast(): return lax.psum(jnp.where(mine, x, jnp.zeros_like(x)), axis)  70.3 us
    all_gather x1, waiting for transfers between devices, local(): lax.all_gather(left_ready, 'blk', axis=0, tiled=True)  60.6 us
    psum x1, waiting for transfers between devices, local(): lax.psum(right_coeffs.astype(jnp.bfloat16), 'grp').astype(jnp.float32)  53.4 us
    psum x1, blocking collectives, local(): lax.psum(left_coeffs.astype(jnp.bfloat16), 'grp').astype(jnp.float32)  44.7 us
    dot_general x4, matrix products, contract(): lax.dot_general(row_block, factors, (((1,), (1,)), ((), ())), preferred_e...  24.2 us
  transfers between devices with their start and end apart: 5, of which 5 were waited for; matrix products, arithmetic and copies ran while one was open for 1% of the time, Pallas kernels for 0%

commit v1 on v0

--- a/solution.py
+++ b/solution.py
@@ -70,7 +70,9 @@
     slot_count = activations.shape[0]
     pieces = (
         lax.all_gather(left_ready, "blk", axis=0, tiled=True),
-        lax.all_gather(right_ready, "blk", axis=0, tiled=True),
+        jnp.concatenate(
+            lax.all_to_all(jnp.stack([right_ready] * lax.axis_size("blk")), "blk", 0, 0), axis=0
+        ),
     )
     left_piece = pieces[0].reshape(-1, pieces[0].shape[2])
     right_piece = pieces[1].reshape(-1, pieces[1].shape[2])

time: 945 us -> 1170 us (1.24)
  blocking collectives: 115 us -> 349 us
  waiting for transfers between devices: 777 us -> 754 us
    psum x1, blocking collectives: 44.7 us -> 279 us  [local(): lax.psum(left_coeffs.astype(jnp.bfloat16), 'grp').astype(jnp.float32)]
    all_gather x1 -> x0, waiting for transfers between devices: 83.8 us -> none  [local(): lax.all_gather(right_ready, 'blk', axis=0, tiled=True)]
    psum x1, waiting for transfers between devices: 53.4 us -> 99.5 us  [local(): lax.psum(right_coeffs.astype(jnp.bfloat16), 'grp').astype(jnp.float32)]
    all_gather x1, waiting for transfers between devices: 60.6 us -> 77.5 us  [local(): lax.all_gather(left_ready, 'blk', axis=0, tiled=True)]
  transfers between devices with their start and end apart: 5 -> 5, of which waited for: 5 -> 4; matrix products, arithmetic and copies ran while one was open for 1% -> 1% of each run, Pallas kernels for 0% -> 0%
where the time goes in v1:
time: 1170 us
  waiting for transfers between devices  754 us (64%)
  blocking collectives  349 us (30%)
  matrix products  28.5 us (2%)
  between operations  14.5 us (1%)
    psum x1, waiting for transfers between devices, local(): lax.psum(new_right.astype(jnp.bfloat16), 'grp').astype(jnp.float32)  349 us
    psum x1, blocking collectives, local(): lax.psum(left_coeffs.astype(jnp.bfloat16), 'grp').astype(jnp.float32)  279 us
    psum x1, waiting for transfers between devices, broadcast(): return lax.psum(jnp.where(mine, x, jnp.zeros_like(x)), axis)  228 us
    psum x1, waiting for transfers between devices, local(): lax.psum(right_coeffs.astype(jnp.bfloat16), 'grp').astype(jnp.float32)  99.5 us
    all_gather x1, waiting for transfers between devices, local(): lax.all_gather(left_ready, 'blk', axis=0, tiled=True)  77.5 us
    psum x1, blocking collectives, broadcast(): return lax.psum(jnp.where(mine, x, jnp.zeros_like(x)), axis)  70.3 us
    dot_general x4, matrix products, contract(): lax.dot_general(row_block, factors, (((1,), (1,)), ((), ())), preferred_e...  23.5 us
  transfers between devices with their start and end apart: 5, of which 4 were waited for; matrix products, arithmetic and copies ran while one was open for 1% of the time, Pallas kernels for 0%

profile of v1, /device:TPU:1, one launch (start us, length us, event | category | flops | bytes accessed | tf_op | source)
XLA Modules:
  0.0 1172.2 jit_solution(6634707646758219344)
XLA Ops:
  6.5 1.4 fusion.15
  9.2 2.1 select_bitcast_fusion
  11.3 0.8 select_bitcast_fusion.1
  12.2 0.0 all-reduce.7.cloned.1.call-start
  12.3 70.3 %all-reduce = (bf16[512]{0:T(512)(128)(2,1)S(1)}, bf16[256]{0:T(256)(128)(2,1)S(1)}) all-reduce(bf16[512]{0:T(512)(128)(2,1)S(1)} %fusion.13, bf16[256]{0:T(256)(128)(2,1)S(1)} %fusion.14), channel_id=1, replica_groups=mesh['blk'=32,'grp'=8] {'blk'}, use_global_device_ids=true, to_apply=%region_7.8 | all-reduce | flops 768 | bytes 3072 | tf_op jit(solution)/shard_map/psum | solution.py:9
  82.6 227.5 %all-reduce.9.cloned.1.call-done = (bf16[3584,512]{1,0:T(8,128)(2,1)}, bf16[1024,256]{1,0:T(8,128)(2,1)}) async-done(((bf16[3584,512]{1,0:T(8,128)(2,1)}, bf16[1024,256]{1,0:T(8,128)(2,1)}), (bf16[3584,512]{1,0:T(8,128)(2,1)}, bf16[1024,256]{1,0:T(8,128)(2,1)})) %all-reduce.9.cloned.1.call-update) | async-done | bytes 4194320 | tf_op jit(solution)/shard_map/psum | solution.py:9
  310.1 3.8 fusion.4
  314.0 99.5 %all-reduce.7.cloned.1.call-done = bf16[64,512]{0,1:T(8,128)(2,1)} async-done(((bf16[64,512]{0,1:T(8,128)(2,1)}), bf16[64,512]{0,1:T(8,128)(2,1)}) %all-reduce.7.cloned.1.call-update) | async-done | bytes 65552 | tf_op jit(solution)/shard_map/psum | solution.py:64
  413.5 3.5 fusion
  417.0 7.0 stack.3
  424.0 11.0 all-to-all-start
  435.0 0.0 all-gather.2.cloned.1.call-start
  435.1 0.3 fusion.5
  435.4 278.8 %psum.57 = bf16[64,256]{0,1:T(8,128)(2,1)S(1)} all-reduce(bf16[64,256]{0,1:T(8,128)(2,1)S(1)} %fusion.5), channel_id=1, replica_groups=mesh['blk'=32,'grp'=8] {'grp'}, use_global_device_ids=true, to_apply=%region_2.3 | all-reduce | flops 16384 | bytes 65536 | tf_op jit(solution)/shard_map/psum | solution.py:63
  714.3 1.0 fusion.3
  715.3 0.0 all-reduce.11.cloned.1.call-start
  715.4 77.5 %all-gather.2.cloned.1.call-done = bf16[64,32,1024]{2,1,0:T(8,128)(2,1)} async-done(((bf16[2,32,1024]{2,1,0:T(8,128)(2,1)}), bf16[64,32,1024]{2,1,0:T(8,128)(2,1)}) %all-gather.2.cloned.1.call-update) | async-done | bytes 4194320 | tf_op jit(solution)/shard_map/all_gather | solution.py:72
  792.8 5.9 fusion.2
  798.7 13.1 %fusion.1 = bf16[512,2048]{0,1:T(8,128)(2,1)} fusion(bf16[2048,3584]{1,0:T(8,128)(2,1)} %bitcast.14, bf16[512,3584]{1,0:T(8,128)(2,1)} %param.11), kind=kOutput, calls=%fused_computation.7 | convolution fusion | flops 7517241344 | bytes 20447232 | tf_op jit(solution)/shard_map/dot_general | solution.py:13
  811.8 0.6 copy-done.7
  812.5 0.2 reduce-window.8
  812.7 348.9 %all-reduce.11.cloned.1.call-done = (bf16[512,2048]{0,1:T(8,128)(2,1)}, bf16[512,2048]{0,1:T(8,128)(2,1)}) async-done(((bf16[512,2048]{0,1:T(8,128)(2,1)}, bf16[512,2048]{0,1:T(8,128)(2,1)}), (bf16[512,2048]{0,1:T(8,128)(2,1)}, bf16[512,2048]{0,1:T(8,128)(2,1)})) %all-reduce.11.cloned.1.call-update) | async-done | bytes 4194320 | tf_op jit(solution)/shard_map/psum | solution.py:84
  1161.6 3.3 bitcast_reduce_fusion
  1164.9 0.8 fusion.9
  (26 shorter events, 0.2 us)
Async XLA Ops:
  6.5 786.3 %copy-start = (bf16[512,1024]{1,0:T(8,128)(2,1)S(1)}, bf16[512,1024]{1,0:T(8,128)(2,1)}, u32[]{:S(2)}) copy-start(bf16[512,1024]{1,0:T(8,128)(2,1)} %param.10) | copy-start | bytes 3145732
  6.5 303.6 %all-reduce.9.cloned.1.call-start = ((), (), s32[]{:S(2)}) async-start(), calls=%async_computation.3 | async-start | bytes 8388608 | tf_op jit(solution)/shard_map/psum | solution.py:9
  9.2 2.1 copy-start.2
  11.3 0.9 copy-start.6
  11.3 0.9 copy-start.5
  11.3 298.8 %copy-start.4 = (bf16[2,32,3584]{2,1,0:T(8,128)(2,1)S(1)}, bf16[2,32,3584]{2,1,0:T(8,128)(2,1)}, u32[]{:S(2)}) copy-start(bf16[2,32,3584]{2,1,0:T(8,128)(2,1)} %param.13) | copy-start | bytes 1376260
  12.2 401.4 %all-reduce.7.cloned.1.call-start = ((), (), s32[]{:S(2)}) async-start(), calls=%async_computation.2 | async-start | bytes 262144 | tf_op jit(solution)/shard_map/psum | solution.py:64
  424.0 11.1 copy-start.1
  424.0 11.1 copy-start.3
  424.0 374.8 %all-to-all-start = ((bf16[32,2,32,3584]{3,2,1,0:T(8,128)(2,1)}), bf16[32,2,32,3584]{3,2,1,0:T(8,128)(2,1)}, u32[]{:S(2)}, u32[]{:S(2)}) async-start(bf16[32,2,32,3584]{3,2,1,0:T(8,128)(2,1)} %stack.3), calls=%async_computation | async-start | bytes 29360128 | tf_op jit(solution)/shard_map/all_to_all | solution.py:74
  435.0 357.8 %all-gather.2.cloned.1.call-start = ((), (), s32[]{:S(2)}) async-start(), calls=%async_computation.1 | async-start | bytes 4325376 | tf_op jit(solution)/shard_map/all_gather | solution.py:72
  715.3 446.3 %all-reduce.11.cloned.1.call-start = ((), (), s32[]{:S(2)}) async-start(), calls=%async_computation.4 | async-start | bytes 8388608 | tf_op jit(solution)/shard_map/psum | solution.py:84
  811.8 0.7 copy-start.7
Sparse Core Ops, SparseCore 0:
  12.3 297.7 all-reduce.8
  314.1 99.3 all-reduce.6
  715.4 77.3 all-gather.1
  812.0 349.5 all-reduce.10
